TPU v7x, 512 devices: a whole 4x4x16 slice. The times are simulated.
512 devices in a mesh: leaf: 128 (over z, x, core), vec: 4 (over y).
Axes of the slice: x: 4, y: 4, z: 16, core: 2. Of those that a mesh axis runs over, the one named last changes fastest.
Arguments:
- samples: bfloat16 [64, 524288], P('vec', 'leaf'), may hold values from -6 to 6
- coords: float32 [3, 524288], P(None, 'leaf'), may hold values from -4 to 4
- panel_area: float32 [524288], P('leaf'), may hold values from 0.05 to 0.5
- quad_weight: float32 [524288], P('leaf'), may hold values from 0.2 to 1
- leaf_basis: bfloat16 [2048, 64, 256], P('leaf'), may hold values from -0.375 to 0.375
- transfer: bfloat16 [1024, 2, 64, 64], P('leaf'), may hold values from -0.5 to 0.5
- coupling_fine: bfloat16 [2048, 16, 64, 64], P('leaf'), may hold values from -0.1875 to 0.1875
- coupling_coarse: bfloat16 [1024, 16, 64, 64], P('leaf'), may hold values from -0.1875 to 0.1875
- near_list: int32 [2048, 16], P('leaf'), may hold values from 0 to 2047, as said below
- send_fine: int32 [16384, 2], P('leaf'), may hold values from 0 to 15
- send_coarse: int32 [16384, 1], P('leaf'), may hold values from 0 to 7
- far_fine: int32 [2048, 16], P('leaf'), may hold values from 0 to 255, as said below
- far_coarse: int32 [1024, 16], P('leaf'), may hold values from 0 to 127, as said below
Outputs:
- sample_out: bfloat16 [64, 524288], P('vec', 'leaf')
- sample_gram: float32 [2048, 64, 64], P('leaf', 'vec')
Inputs may be any that keep to these rules, and one draw needn't show every extreme that they name: `near_list`: row g names 16 different leaves, each at most 16 leaves from g. `send_fine`: row e * 128 + d names clusters of device e, counted on e from 0; every slot carries one. `send_coarse`: row e * 128 + d names clusters of device e, counted on e from 0; every slot carries one. `far_fine`: the rows of one device's 16 leaves name each of the values 0 to 255 exactly once. `far_coarse`: the rows of one device's parents name each of the values 0 to 127 exactly once.
All inputs are finite; a program needn't handle non-finite values.
Results may differ from a plain program's by a relative error of at most 0.0085.
Values may be sent and summed in bfloat16 or wider, within the bound.
No kernel may reach another device: no remote copies, remote signals or barrier semaphores. Data moves between devices by JAX's collectives and lax.ppermute only.
A program may use at most 64 MiB of HBM per device.

v0:
```python
import jax
import jax.numpy as jnp
from jax import lax
from jax.sharding import PartitionSpec as P

LEAF = 256
HW = 16


four_pi = 4.0 * 3.141592653589793


def extended(block, sides, width):
    for axis, dim in sides:
        count = lax.axis_size(axis)
        forward = [(i, i + 1) for i in range(count - 1)]
        backward = [(target, source) for source, target in forward]
        low = lax.ppermute(
            lax.slice_in_dim(block, block.shape[dim] - width, None, axis=dim), axis, forward
        )
        high = lax.ppermute(lax.slice_in_dim(block, 0, width, axis=dim), axis, backward)
        block = jnp.concatenate([low, block, high], axis=dim)
    return block


def laid_out(blocks, dim):
    dims = list(blocks.shape[1:])
    dims[dim] *= blocks.shape[0]
    return jnp.moveaxis(blocks, 0, dim).reshape(dims)


def copy_for_each(array, axis):
    copies = jnp.broadcast_to(array, (lax.axis_size(axis), *array.shape))
    return lax.all_to_all(copies, axis, split_axis=0, concat_axis=0, tiled=True)


def gathered_copies(array, axis, dim):
    return laid_out(copy_for_each(array, axis), dim)


def kernel_block(target, source):
    delta_x = target[0][:, None] - source[0][None, :]
    delta_y = target[1][:, None] - source[1][None, :]
    delta_z = target[2][:, None] - source[2][None, :]
    distance = delta_x * delta_x + delta_y * delta_y + delta_z * delta_z + source[3][None, :]
    return (source[4][None, :] / (four_pi * jnp.sqrt(distance))).astype(jnp.bfloat16)


def apply_coupling(tile_set, received, far_list, vec_dev, basis_rank):
    coef_table = received.reshape(-1, vec_dev, basis_rank)
    picked = coef_table[far_list]
    return jnp.einsum("ibkl,ibvl->ivk", tile_set, picked, preferred_element_type=jnp.float32)


def near_leaves(leaf_ids, window, geo_leaves, vec_leaves, targets):

    def one_leaf(index):
        chosen = window[index]
        src_geo = jnp.take(geo_leaves, chosen, axis=1)
        src_vec = jnp.take(vec_leaves, chosen, axis=1)
        target = lax.dynamic_index_in_dim(targets, index, 1, keepdims=False)
        blocks = jax.vmap(kernel_block, (None, 1))(target, src_geo)
        return jnp.einsum("npq,vnq->vp", blocks, src_vec, preferred_element_type=jnp.float32)

    return lax.map(one_leaf, leaf_ids)


def per_device(
    samples,
    coords,
    panel_area,
    quad_weight,
    leaf_basis,
    transfer,
    coupling_fine,
    coupling_coarse,
    near_list,
    send_fine,
    send_coarse,
    far_fine,
    far_coarse,
):
    vec_dev, points = samples.shape
    leaf_dev, basis_rank, leaf_pts = leaf_basis.shape
    devices = lax.axis_size("leaf")
    device = lax.axis_index("leaf")
    geometry = jnp.concatenate([coords, panel_area[None, :], quad_weight[None, :]], axis=0)
    geo_wide = extended(geometry, (("leaf", 1),), HW * leaf_pts)
    vec_wide = extended(samples, (("leaf", 1),), HW * leaf_pts)
    geo_leaves = geo_wide.reshape(5, -1, leaf_pts)
    window = near_list - (device * leaf_dev - HW)
    targets = coords.reshape(3, leaf_dev, leaf_pts)
    local_rows = samples.reshape(vec_dev, leaf_dev, leaf_pts)
    fine_coef = jnp.einsum(
        "ikp,vip->ivk", leaf_basis, local_rows, preferred_element_type=jnp.float32
    ).astype(jnp.bfloat16)
    coarse_coef = jnp.einsum(
        "mskl,msvk->mvl",
        transfer,
        fine_coef.reshape(-1, 2, vec_dev, basis_rank),
        preferred_element_type=jnp.float32,
    ).astype(jnp.bfloat16)
    send_leafs = fine_coef[send_fine].reshape(devices, -1, vec_dev * basis_rank)
    send_parents = coarse_coef[send_coarse].reshape(devices, -1, vec_dev * basis_rank)
    got_leafs = lax.all_to_all(send_leafs, "leaf", split_axis=0, concat_axis=0, tiled=True)
    got_parents = lax.all_to_all(send_parents, "leaf", split_axis=0, concat_axis=0, tiled=True)
    vec_groups = lax.axis_size("vec")
    quarter = leaf_dev // vec_groups
    all_wide = gathered_copies(vec_wide, "vec", 0)
    all_leaves = all_wide.reshape(all_wide.shape[0], -1, leaf_pts)
    first_leaf = lax.axis_index("vec") * quarter
    leaf_ids = first_leaf + jnp.arange(quarter, dtype=jnp.int32)
    near_quarter = near_leaves(leaf_ids, window, geo_leaves, all_leaves, targets)
    near_part = lax.all_to_all(
        near_quarter.astype(jnp.bfloat16), "vec", split_axis=1, concat_axis=0, tiled=True
    ).astype(near_quarter.dtype)
    field_fine = apply_coupling(coupling_fine, got_leafs, far_fine, vec_dev, basis_rank)
    field_coarse = apply_coupling(
        coupling_coarse, got_parents, far_coarse, vec_dev, basis_rank
    ).astype(jnp.bfloat16)
    pushed = jnp.einsum(
        "mskl,mvl->msvk", transfer, field_coarse, preferred_element_type=jnp.float32
    )
    local_field = (field_fine + pushed.reshape(leaf_dev, vec_dev, basis_rank)).astype(jnp.bfloat16)
    far_part = jnp.einsum(
        "ikp,ivk->vip", leaf_basis, local_field, preferred_element_type=jnp.float32
    )
    sample_out = (
        (jnp.transpose(near_part, (1, 0, 2)) + far_part)
        .reshape(vec_dev, points)
        .astype(jnp.bfloat16)
    )
    own_rows = sample_out.reshape(vec_dev, leaf_dev, leaf_pts)
    shard_rows = gathered_copies(sample_out, "vec", 0)
    shaped = shard_rows.reshape(shard_rows.shape[0], leaf_dev, leaf_pts)
    sample_gram = jnp.einsum(
        "vip,wip->ivw", own_rows, shaped, preferred_element_type=jnp.float32
    ) * (1.0 / LEAF)
    return (sample_out, sample_gram)


def solution(mesh):
    return jax.shard_map(
        per_device,
        mesh=mesh,
        in_specs=(
            P("vec", "leaf"),
            P(None, "leaf"),
            P("leaf"),
            P("leaf"),
            P("leaf", None, None),
            P("leaf", None, None, None),
            P("leaf", None, None, None),
            P("leaf", None, None, None),
            P("leaf", None),
            P("leaf", None),
            P("leaf", None),
            P("leaf", None),
            P("leaf", None),
        ),
        out_specs=(P("vec", "leaf"), P("leaf", "vec", None)),
        check_vma=False,
    )
```

profile of v0, /device:TPU:32, one launch (start us, length us, event | category | flops | bytes accessed | tf_op | source)
XLA Modules:
  0.0 212.3 jit_solution(4894522826093835305)
XLA Ops:
  0.7 3.8 %collective-permute-start.1 = (bf16[16,4096]{1,0:T(8,128)(2,1)}, bf16[16,4096]{1,0:T(8,128)(2,1)}, u32[]{:S(2)}, u32[]{:S(2)}) collective-permute-start(bf16[16,4096]{1,0:T(8,128)(2,1)} %param.15), channel_id=1, source_target_pairs={{4,0},{8,4},{12,8},{16,12},{20,16},{24,20},{28,24},{32,28},{36,32}... | collective-permute-start | bytes 393224 | tf_op jit(solution)/shard_map/ppermute | solution.py:21
  4.5 1.9 collective-permute-start
  7.3 5.8 %collective-permute-start.3 = (f32[5,4096]{1,0:T(8,128)S(1)}, f32[5,4096]{1,0:T(8,128)S(1)}, u32[]{:S(2)}, u32[]{:S(2)}) collective-permute-start(f32[5,4096]{1,0:T(8,128)S(1)} %pad_maximum_fusion.2), channel_id=1, source_target_pairs={{4,0},{8,4},{12,8},{16,12},{20,16},{24,20},{28,24},{32,28},{36,32}... | collective-permute-start | bytes 245768 | tf_op jit(solution)/shard_map/ppermute | solution.py:21
  13.1 1.9 collective-permute-start.2
  28.8 4.5 %all-to-all-start = ((bf16[4,16,12288]{2,1,0:T(8,128)(2,1)}), bf16[4,16,12288]{2,1,0:T(8,128)(2,1)}, u32[]{:S(2)}, u32[]{:S(2)}) async-start(bf16[4,16,12288]{2,1,0:T(8,128)(2,1)} %broadcast_in_dim.52), calls=%async_computation | async-start | bytes 3145728 | tf_op jit(solution)/shard_map/all_to_all | solution.py:34
  34.3 17.8 %all-to-all-done = bf16[4,16,12288]{2,1,0:T(8,128)(2,1)} async-done(((bf16[4,16,12288]{2,1,0:T(8,128)(2,1)}), bf16[4,16,12288]{2,1,0:T(8,128)(2,1)}, u32[]{:S(2)}, u32[]{:S(2)}) %all-to-all-start) | async-done | bytes 1572896 | tf_op jit(solution)/shard_map/all_to_all | solution.py:34
  52.1 19.6 %all-to-all-start.3 = ((bf16[128,2,512]{2,1,0:T(2,128)(2,1)}), bf16[128,2,512]{2,1,0:T(2,128)(2,1)S(1)}, u32[]{:S(2)}, u32[]{:S(2)}) async-start(bf16[128,2,512]{2,1,0:T(2,128)(2,1)} %reshape.159), calls=%async_computation.3 | async-start | bytes 524288 | tf_op jit(solution)/shard_map/all_to_all | solution.py:106
  75.2 54.8 %while.10 = (s32[]{:T(128)}, bf16[4,64,256]{2,0,1:T(4,128)(2,1)}, s32[4]{0:T(128)}, s32[16,16]{1,0:T(8,128)}, bf16[64,48,256]{2,0,1:T(8,128)(2,1)}, /*index=5*/f...) while((s32[]{:T(128)}, bf16[4,64,256]{2,0,1:T(4,128)(2,1)}, ...), condition=%wide.region_1.2_spmd, body=%wide.region_0.1_spmd.sunk | while | flops 147084432 | bytes 3536671 | solution.py:65
  81.7 2.0 gather_fusion.1
  83.7 3.6 %fusion.38 = bf16[1,64,256]{2,1,0:T(8,128)(2,1)S(1)} fusion(f32[16,256]{1,0:T(8,128)S(1)} %get-tuple-element.137, f32[16,256]{1,0:T(8,128)S(1)} %get-tuple-element.138, f32[256]{0:T(256)} %bitcast.153, f32[16,256]{1,0:T(8,128)S(1)} %get-tuple-element.142, f32[256]{0:T(256)} %bitcast.152, f32[16,256]{1,0:T(8,128)S(1)} %get-tuple-element.144, ...), kind=kOutput, calls=%fused_computation.8.clone.1 | convolution fusion | flops 147062784 | bytes 642064 | tf_op jit(solution)/shard_map/while/body/eval_jaxpr/npq,vnq->vp/dot_general | solution.py:63
  95.4 2.0 gather_fusion.1
  97.4 3.6 %fusion.38 = bf16[1,64,256]{2,1,0:T(8,128)(2,1)S(1)} fusion(f32[16,256]{1,0:T(8,128)S(1)} %get-tuple-element.137, f32[16,256]{1,0:T(8,128)S(1)} %get-tuple-element.138, f32[256]{0:T(256)} %bitcast.153, f32[16,256]{1,0:T(8,128)S(1)} %get-tuple-element.142, f32[256]{0:T(256)} %bitcast.152, f32[16,256]{1,0:T(8,128)S(1)} %get-tuple-element.144, ...), kind=kOutput, calls=%fused_computation.8.clone.1 | convolution fusion | flops 147062784 | bytes 642064 | tf_op jit(solution)/shard_map/while/body/eval_jaxpr/npq,vnq->vp/dot_general | solution.py:63
  109.1 2.0 gather_fusion.1
  111.1 3.6 %fusion.38 = bf16[1,64,256]{2,1,0:T(8,128)(2,1)S(1)} fusion(f32[16,256]{1,0:T(8,128)S(1)} %get-tuple-element.137, f32[16,256]{1,0:T(8,128)S(1)} %get-tuple-element.138, f32[256]{0:T(256)} %bitcast.153, f32[16,256]{1,0:T(8,128)S(1)} %get-tuple-element.142, f32[256]{0:T(256)} %bitcast.152, f32[16,256]{1,0:T(8,128)S(1)} %get-tuple-element.144, ...), kind=kOutput, calls=%fused_computation.8.clone.1 | convolution fusion | flops 147062784 | bytes 642064 | tf_op jit(solution)/shard_map/while/body/eval_jaxpr/npq,vnq->vp/dot_general | solution.py:63
  122.8 2.0 gather_fusion.1
  124.8 3.6 %fusion.38 = bf16[1,64,256]{2,1,0:T(8,128)(2,1)S(1)} fusion(f32[16,256]{1,0:T(8,128)S(1)} %get-tuple-element.137, f32[16,256]{1,0:T(8,128)S(1)} %get-tuple-element.138, f32[256]{0:T(256)} %bitcast.153, f32[16,256]{1,0:T(8,128)S(1)} %get-tuple-element.142, f32[256]{0:T(256)} %bitcast.152, f32[16,256]{1,0:T(8,128)S(1)} %get-tuple-element.144, ...), kind=kOutput, calls=%fused_computation.8.clone.1 | convolution fusion | flops 147062784 | bytes 642064 | tf_op jit(solution)/shard_map/while/body/eval_jaxpr/npq,vnq->vp/dot_general | solution.py:63
  130.7 4.1 %all-to-all-start.1 = ((bf16[4,64,256]{2,0,1:T(4,128)(2,1)}), bf16[4,64,256]{2,0,1:T(4,128)(2,1)}, u32[]{:S(2)}, u32[]{:S(2)}) async-start(bf16[4,64,256]{2,0,1:T(4,128)(2,1)} %get-tuple-element.39), calls=%async_computation.1 | async-start | bytes 262144 | tf_op jit(solution)/shard_map/all_to_all | solution.py:114
  137.7 3.2 %all-to-all-done.1 = bf16[4,64,256]{2,0,1:T(4,128)(2,1)} async-done(((bf16[4,64,256]{2,0,1:T(4,128)(2,1)}), bf16[4,64,256]{2,0,1:T(4,128)(2,1)}, u32[]{:S(2)}, u32[]{:S(2)}) %all-to-all-start.1) | async-done | bytes 131104 | tf_op jit(solution)/shard_map/all_to_all | solution.py:114
  140.9 16.6 %all-to-all-start.2 = ((bf16[128,2,1024]{2,1,0:T(2,128)(2,1)}), bf16[128,2,1024]{2,1,0:T(2,128)(2,1)}, u32[]{:S(2)}, u32[]{:S(2)}) async-start(bf16[128,2,1024]{2,1,0:T(2,128)(2,1)} %reshape.89), calls=%async_computation.2 | async-start | bytes 1048576 | tf_op jit(solution)/shard_map/all_to_all | solution.py:105
  157.7 2.2 %reshape.160 = bf16[128,1,1024]{2,1,0:T(2,128)(2,1)S(1)} reshape(bf16[128,2,512]{2,1,0:T(2,128)(2,1)} %copy-done.2) | data formatting | bytes 524288
  163.9 26.2 %all-to-all-done.2 = bf16[128,2,1024]{2,1,0:T(2,128)(2,1)} async-done(((bf16[128,2,1024]{2,1,0:T(2,128)(2,1)}), bf16[128,2,1024]{2,1,0:T(2,128)(2,1)}, u32[]{:S(2)}, u32[]{:S(2)}) %all-to-all-start.2) | async-done | bytes 524320 | tf_op jit(solution)/shard_map/all_to_all | solution.py:105
  190.1 2.3 %reshape.90 = bf16[256,16,64]{2,1,0:T(8,128)(2,1)S(1)} reshape(bf16[128,2,1024]{2,1,0:T(2,128)(2,1)} %all-to-all-done.2) | data formatting | bytes 1048576 | tf_op jit(solution)/shard_map/reshape | solution.py:50
  194.2 4.0 %fusion.9 = bf16[16,16,256]{2,1,0:T(8,128)(2,1)S(1)} fusion(f32[16,16,256]{2,1,0:T(8,128)S(1)} %bitcast.140, bf16[16,64,256]{2,1,0:T(8,128)(2,1)} %param.19, f32[16,16,64]{2,1,0:T(8,128)} %bitcast.142, bf16[16,16,16,64]{3,2,1,0:T(8,128)(2,1)} %bitcast.132, bf16[16,16,64,64]{3,2,1,0:T(8,128)(2,1)} %param.21), kind=kOutput, calls=%fused_computation.31 | convolution fusion | flops 42106880 | bytes 3604480 | tf_op jit(solution)/shard_map/ikp,ivk->vip/dot_general | solution.py:125
  198.2 13.0 %all_to_all.29 = bf16[4,16,4096]{2,1,0:T(8,128)(2,1)S(1)} all-to-all(bf16[4,16,4096]{2,1,0:T(8,128)(2,1)S(1)} %broadcast_in_dim.59), channel_id=1, replica_groups=mesh['leaf'=128,'vec'=4] {'vec'}, dimensions={0} | all-to-all | bytes 1048576 | tf_op jit(solution)/shard_map/all_to_all | solution.py:34
  (141 shorter events, 54.9 us)
Async XLA Ops:
  0.6 160.8 %copy-start = (bf16[8,16,64,64]{3,2,1,0:T(8,128)(2,1)S(1)}, bf16[8,16,64,64]{3,2,1,0:T(8,128)(2,1)}, u32[]{:S(2)}) copy-start(bf16[8,16,64,64]{3,2,1,0:T(8,128)(2,1)} %param.22) | copy-start | bytes 3145732
  0.6 25.9 %copy-start.5 = (bf16[16,4096]{1,0:T(8,128)(2,1)S(1)}, bf16[16,4096]{1,0:T(8,128)(2,1)}, u32[]{:S(2)}) copy-start(bf16[16,4096]{1,0:T(8,128)(2,1)} %param.15) | copy-start | bytes 393220
  0.7 25.9 %collective-permute-start.1 = (bf16[16,4096]{1,0:T(8,128)(2,1)}, bf16[16,4096]{1,0:T(8,128)(2,1)}, u32[]{:S(2)}, u32[]{:S(2)}) collective-permute-start(bf16[16,4096]{1,0:T(8,128)(2,1)} %param.15), channel_id=1, source_target_pairs={{4,0},{8,4},{12,8},{16,12},{20,16},{24,20},{28,24},{32,28},{36,32}... | collective-permute-start | bytes 393224 | tf_op jit(solution)/shard_map/ppermute | solution.py:21
  4.5 22.1 %collective-permute-start = (bf16[16,4096]{1,0:T(8,128)(2,1)}, bf16[16,4096]{1,0:T(8,128)(2,1)}, u32[]{:S(2)}, u32[]{:S(2)}) collective-permute-start(bf16[16,4096]{1,0:T(8,128)(2,1)} %param.15), channel_id=1, source_target_pairs={{0,4},{4,8},{8,12},{12,16},{16,20},{20,24},{24,28},{28,32},{32,36}... | collective-permute-start | bytes 393224 | tf_op jit(solution)/shard_map/ppermute | solution.py:18
  7.3 25.9 %collective-permute-start.3 = (f32[5,4096]{1,0:T(8,128)S(1)}, f32[5,4096]{1,0:T(8,128)S(1)}, u32[]{:S(2)}, u32[]{:S(2)}) collective-permute-start(f32[5,4096]{1,0:T(8,128)S(1)} %pad_maximum_fusion.2), channel_id=1, source_target_pairs={{4,0},{8,4},{12,8},{16,12},{20,16},{24,20},{28,24},{32,28},{36,32}... | collective-permute-start | bytes 245768 | tf_op jit(solution)/shard_map/ppermute | solution.py:21
  13.1 20.2 %collective-permute-start.2 = (f32[5,4096]{1,0:T(8,128)S(1)}, f32[5,4096]{1,0:T(8,128)}, u32[]{:S(2)}, u32[]{:S(2)}) collective-permute-start(f32[5,4096]{1,0:T(8,128)S(1)} %pad_maximum_fusion.2), channel_id=1, source_target_pairs={{0,4},{4,8},{8,12},{12,16},{16,20},{20,24},{24,28},{28,32},{32,36}... | collective-permute-start | bytes 245768 | tf_op jit(solution)/shard_map/ppermute | solution.py:18
  22.4 10.9 %copy-start.3 = (f32[3,4096]{1,0:T(4,128)S(1)}, f32[3,4096]{1,0:T(4,128)}, u32[]{:S(2)}) copy-start(f32[3,4096]{1,0:T(4,128)} %param.16) | copy-start | bytes 147460
  22.4 10.9 %copy-start.8 = (f32[4096]{0:T(1024)S(1)}, f32[4096]{0:T(1024)}, u32[]{:S(2)}) copy-start(f32[4096]{0:T(1024)} %param.18) | copy-start | bytes 49156
  28.8 23.3 %all-to-all-start = ((bf16[4,16,12288]{2,1,0:T(8,128)(2,1)}), bf16[4,16,12288]{2,1,0:T(8,128)(2,1)}, u32[]{:S(2)}, u32[]{:S(2)}) async-start(bf16[4,16,12288]{2,1,0:T(8,128)(2,1)} %broadcast_in_dim.52), calls=%async_computation | async-start | bytes 3145728 | tf_op jit(solution)/shard_map/all_to_all | solution.py:34
  52.1 77.9 %all-to-all-start.3 = ((bf16[128,2,512]{2,1,0:T(2,128)(2,1)}), bf16[128,2,512]{2,1,0:T(2,128)(2,1)S(1)}, u32[]{:S(2)}, u32[]{:S(2)}) async-start(bf16[128,2,512]{2,1,0:T(2,128)(2,1)} %reshape.159), calls=%async_computation.3 | async-start | bytes 524288 | tf_op jit(solution)/shard_map/all_to_all | solution.py:106
  80.1 1.5 copy-start.9
  83.7 3.7 %copy-start.6 = (bf16[4,64,256]{2,0,1:T(4,128)(2,1)S(1)}, bf16[4,64,256]{2,0,1:T(4,128)(2,1)}, u32[]{:S(2)}) copy-start(bf16[4,64,256]{2,0,1:T(4,128)(2,1)} %get-tuple-element.160) | copy-start | bytes 393220 | tf_op jit(solution)/shard_map/while
  93.8 1.5 copy-start.9
  97.4 3.7 %copy-start.6 = (bf16[4,64,256]{2,0,1:T(4,128)(2,1)S(1)}, bf16[4,64,256]{2,0,1:T(4,128)(2,1)}, u32[]{:S(2)}) copy-start(bf16[4,64,256]{2,0,1:T(4,128)(2,1)} %get-tuple-element.160) | copy-start | bytes 393220 | tf_op jit(solution)/shard_map/while
  107.5 1.5 copy-start.9
  111.1 3.7 %copy-start.6 = (bf16[4,64,256]{2,0,1:T(4,128)(2,1)S(1)}, bf16[4,64,256]{2,0,1:T(4,128)(2,1)}, u32[]{:S(2)}) copy-start(bf16[4,64,256]{2,0,1:T(4,128)(2,1)} %get-tuple-element.160) | copy-start | bytes 393220 | tf_op jit(solution)/shard_map/while
  121.2 1.5 copy-start.9
  124.8 3.7 %copy-start.6 = (bf16[4,64,256]{2,0,1:T(4,128)(2,1)S(1)}, bf16[4,64,256]{2,0,1:T(4,128)(2,1)}, u32[]{:S(2)}) copy-start(bf16[4,64,256]{2,0,1:T(4,128)(2,1)} %get-tuple-element.160) | copy-start | bytes 393220 | tf_op jit(solution)/shard_map/while
  130.0 27.4 %copy-start.11 = (s32[8,16]{1,0:T(8,128)S(1)}, s32[8,16]{1,0:T(8,128)}, u32[]{:S(2)}) copy-start(s32[8,16]{1,0:T(8,128)} %param.27) | copy-start | bytes 1540
  130.0 27.5 %copy-start.10 = (s32[16,16]{1,0:T(8,128)S(1)}, s32[16,16]{1,0:T(8,128)}, u32[]{:S(2)}) copy-start(s32[16,16]{1,0:T(8,128)} %param.26) | copy-start | bytes 3076
  130.7 30.7 %copy-start.1 = (bf16[8,2,64,64]{3,2,1,0:T(8,128)(2,1)S(1)}, bf16[8,2,64,64]{3,2,1,0:T(8,128)(2,1)}, u32[]{:S(2)}) copy-start(bf16[8,2,64,64]{3,2,1,0:T(8,128)(2,1)} %param.20) | copy-start | bytes 393220
  130.7 10.1 %all-to-all-start.1 = ((bf16[4,64,256]{2,0,1:T(4,128)(2,1)}), bf16[4,64,256]{2,0,1:T(4,128)(2,1)}, u32[]{:S(2)}, u32[]{:S(2)}) async-start(bf16[4,64,256]{2,0,1:T(4,128)(2,1)} %get-tuple-element.39), calls=%async_computation.1 | async-start | bytes 262144 | tf_op jit(solution)/shard_map/all_to_all | solution.py:114
  140.9 49.3 %all-to-all-start.2 = ((bf16[128,2,1024]{2,1,0:T(2,128)(2,1)}), bf16[128,2,1024]{2,1,0:T(2,128)(2,1)}, u32[]{:S(2)}, u32[]{:S(2)}) async-start(bf16[128,2,1024]{2,1,0:T(2,128)(2,1)} %reshape.89), calls=%async_computation.2 | async-start | bytes 1048576 | tf_op jit(solution)/shard_map/all_to_all | solution.py:105
  198.2 14.1 %copy-start.4 = (bf16[16,2,8,256]{3,2,0,1:T(8,128)(2,1)}, bf16[16,2,8,256]{3,2,0,1:T(8,128)(2,1)S(1)}, u32[]{:S(2)}) copy-start(bf16[16,2,8,256]{3,2,0,1:T(8,128)(2,1)S(1)} %copy.55) | copy-start | bytes 393220
  (5 other events, 3.3 us)
where the time goes:
time: 214 us; the launch traced here: 212 us
  starting transfers between devices  58.1 us (27%)
  local copies, waits for them, and re-layouts  48.9 us (23%)
  waiting for transfers between devices  47.2 us (22%)
  matrix products  23.4 us (11%)
  other arithmetic  13.4 us (6%)
  blocking collectives  13 us (6%)
  loops' own time  7.29 us (3%)
    all_to_all x1, waiting for transfers between devices, per_device(): lax.all_to_all(send_leafs, 'leaf', split_axis=0, concat_axis=0, tiled=True)  26.2 us
    all_to_all x1, starting transfers between devices, per_device(): lax.all_to_all(send_parents, 'leaf', split_axis=0, concat_axis=0, tiled=T...  19.6 us
    all_to_all x1, waiting for transfers between devices, copy_for_each(): return lax.all_to_all(copies, axis, split_axis=0, concat_axis=0, tiled=True)  17.8 us
    all_to_all x1, starting transfers between devices, per_device(): lax.all_to_all(send_leafs, 'leaf', split_axis=0, concat_axis=0, tiled=True)  16.6 us
    dot_general x4, matrix products, one_leaf(): jnp.einsum('npq,vnq->vp', blocks, src_vec, preferred_element_type=jnp.flo...  14.5 us
    all_to_all x1, blocking collectives, copy_for_each(): return lax.all_to_all(copies, axis, split_axis=0, concat_axis=0, tiled=True)  13 us
    ppermute x2, starting transfers between devices, extended(): lax.ppermute(lax.slice_in_dim(block, 0, width, axis=dim), axis, backward)  9.54 us
    gather x4, local copies, waits for them, and re-layouts, one_leaf(): src_vec = jnp.take(vec_leaves, chosen, axis=1)  7.95 us
  transfers between devices with their start and end apart: 8, of which 3 were waited for; matrix products, arithmetic and copies ran while one was open for 34% of the time, Pallas kernels for 0%

commit v1 on v0

v1 whole, which is shorter than its diff:
```python
import jax
import jax.numpy as jnp
from jax import lax
from jax.experimental import pallas as pl
from jax.experimental.pallas import tpu as pltpu
from jax.sharding import PartitionSpec as P

HW = 16
LANES = 128
FEATURES = 16
TERMS = 32
PAIRS = ((0, 0), (0, 1), (1, 0), (1, 1), (0, 2), (2, 0))

bf16 = jnp.bfloat16
f32 = jnp.float32
VM = pl.BlockSpec(memory_space=pltpu.VMEM)
SM = pl.BlockSpec(memory_space=pltpu.SMEM)
NT = (((1,), (1,)), ((), ()))
TN = (((0,), (0,)), ((), ()))


def params(mebibytes):
    return pltpu.CompilerParams(vmem_limit_bytes=mebibytes << 20)


def split3(x):
    hi = x.astype(bf16).astype(f32)
    rest = x - hi
    mid = rest.astype(bf16).astype(f32)
    return [hi, mid, rest - mid]


def term_rows():
    target, source = [], []
    for group in range(4):
        for first, second in PAIRS:
            target.append(3 * group + first)
            source.append((0, 6, 9, 12)[group] + second)
    for part in range(3):
        target.append(12)
        source.append(3 + part)
    return target, source


def selection(chosen, row, column):
    found = jnp.zeros(row.shape, f32)
    for place, index in enumerate(chosen):
        found = jnp.where((row == place) & (column == index), 1.0, found)
    return found.astype(bf16)


def source_kernel(samples_ref, coords_ref, area_ref, weight_ref, out_ref):
    vec_dev = samples_ref.shape[0]
    out_ref[0:vec_dev, :] = samples_ref[...]
    x, y, z = coords_ref[0:1, :], coords_ref[1:2, :], coords_ref[2:3, :]
    weight = weight_ref[...]
    scale = (16.0 * 3.141592653589793**2) / (weight * weight)
    shift = scale * (x * x + y * y + z * z + area_ref[...])
    rows = split3(scale) + split3(shift)
    for axis in (x, y, z):
        rows += split3(-2.0 * scale * axis)
    rows.append(jnp.zeros_like(scale))
    out_ref[vec_dev:, :] = jnp.concatenate(rows, axis=0).astype(bf16)


def source_rows(samples, coords, panel_area, quad_weight):
    vec_dev, points = samples.shape
    return pl.pallas_call(
        source_kernel,
        out_shape=jax.ShapeDtypeStruct((vec_dev + FEATURES, points), bf16),
        in_specs=[VM] * 4,
        out_specs=VM,
        compiler_params=params(6),
        name="source_rows",
    )(samples, coords, panel_area.reshape(1, -1), quad_weight.reshape(1, -1))


def coef_kernel(fine_ref, coarse_ref, samples_ref, basis_ref, transfer_ref, out_ref, table):
    leaf_dev, rank, pts = basis_ref.shape
    half = samples_ref.shape[0] // 2
    devices = fine_ref.shape[1]
    fine = []

    def keep(at, value):
        table[at] = jnp.concatenate([value[:half], value[half:]], axis=1).astype(bf16)

    for leaf in range(leaf_dev):
        value = lax.dot_general(
            samples_ref[:, leaf * pts : (leaf + 1) * pts],
            basis_ref[leaf],
            NT,
            preferred_element_type=f32,
        )
        keep(leaf, value)
        fine.append(value.astype(bf16))
    for parent in range(leaf_dev // 2):
        value = jnp.dot(fine[2 * parent], transfer_ref[parent, 0], preferred_element_type=f32)
        value += jnp.dot(fine[2 * parent + 1], transfer_ref[parent, 1], preferred_element_type=f32)
        keep(leaf_dev + parent, value)

    slots, parents = fine_ref.shape[0], coarse_ref.shape[0]
    width = slots + parents

    def fill(device, carry):
        for s in range(slots):
            out_ref[device * width + s] = table[fine_ref[s, device]]
        for s in range(parents):
            out_ref[device * width + slots + s] = table[leaf_dev + coarse_ref[s, device]]
        return carry

    lax.fori_loop(0, devices, fill, 0, unroll=8)


def send_rows(send_fine, send_coarse, samples, leaf_basis, transfer):
    leaf_dev, rank, _ = leaf_basis.shape
    half = samples.shape[0] // 2
    devices = send_fine.shape[0]
    width = send_fine.shape[1] + send_coarse.shape[1]
    return pl.pallas_call(
        coef_kernel,
        out_shape=jax.ShapeDtypeStruct((devices * width, half, 2 * rank), bf16),
        in_specs=[SM, SM] + [VM] * 3,
        out_specs=VM,
        scratch_shapes=[pltpu.VMEM((leaf_dev + leaf_dev // 2, half, 2 * rank), bf16)],
        compiler_params=params(8),
        name="send_rows",
    )(send_fine.T, send_coarse.T, samples, leaf_basis, transfer)


def near_kernel(first_ref, list_ref, coords_ref, own_ref, low_ref, high_ref, out_ref, feat, vals):
    vec_dev = out_ref.shape[0]
    leaf_dev, partners = list_ref.shape
    pts = feat.shape[2]
    target_rows, source_rows_ = term_rows()
    wide = selection(
        source_rows_,
        lax.broadcasted_iota(jnp.int32, (TERMS, FEATURES), 0),
        lax.broadcasted_iota(jnp.int32, (TERMS, FEATURES), 1),
    )
    tall = selection(
        target_rows,
        lax.broadcasted_iota(jnp.int32, (FEATURES, TERMS), 1),
        lax.broadcasted_iota(jnp.int32, (FEATURES, TERMS), 0),
    )
    for place, part in enumerate((low_ref, own_ref, high_ref)):
        for leaf in range(leaf_dev):
            cols = slice(leaf * pts, (leaf + 1) * pts)
            feat[place * leaf_dev + leaf] = jnp.dot(
                wide, part[vec_dev:, cols], preferred_element_type=f32
            ).astype(bf16)
            vals[place * leaf_dev + leaf] = part[0:vec_dev, cols]

    def one_leaf(leaf, carry):
        cols = pl.ds(pl.multiple_of(leaf * pts, pts), pts)
        x, y, z = coords_ref[0:1, cols], coords_ref[1:2, cols], coords_ref[2:3, cols]
        rows = split3(x * x + y * y + z * z) + split3(x) + split3(y) + split3(z)
        rows += [jnp.ones_like(x)] + [jnp.zeros_like(x)] * 3
        pieces = jnp.concatenate(rows, axis=0).astype(bf16)
        target = lax.dot_general(pieces, tall, TN, preferred_element_type=f32).astype(bf16)
        total = jnp.zeros((pts, vec_dev), f32)
        for n in range(partners):
            at = list_ref[leaf, n] - first_ref[0]
            dist = jnp.dot(target, feat[at], preferred_element_type=f32)
            block = lax.rsqrt(dist.astype(bf16))
            total += lax.dot_general(block, vals[at], NT, preferred_element_type=f32)
        out_ref[:, cols] = total.T
        return carry

    lax.fori_loop(0, leaf_dev, one_leaf, 0)


def near_field(first, near_list, coords, own, low, high, pts):
    vec_dev = own.shape[0] - FEATURES
    leaf_dev, partners = near_list.shape
    points = coords.shape[1]
    pairs = leaf_dev * partners * pts * pts
    return pl.pallas_call(
        near_kernel,
        out_shape=jax.ShapeDtypeStruct((vec_dev, points), f32),
        in_specs=[SM, SM] + [VM] * 4,
        out_specs=VM,
        scratch_shapes=[
            pltpu.VMEM((3 * leaf_dev, TERMS, pts), bf16),
            pltpu.VMEM((3 * leaf_dev, vec_dev, pts), bf16),
        ],
        compiler_params=params(8),
        cost_estimate=pl.CostEstimate(
            flops=2 * 512 * pairs, transcendentals=pairs, bytes_accessed=4 << 20
        ),
        name="near_field",
    )(first, near_list, coords, own, low, high)


def far_kernel(
    fine_list_ref,
    coarse_list_ref,
    got_ref,
    fine_ref,
    coarse_ref,
    transfer_ref,
    basis_ref,
    near_ref,
    out_ref,
    copies_ref,
):
    leaf_dev, partners = fine_list_ref.shape
    width = 3
    rank, pts = basis_ref.shape[1:]

    def field(tiles_ref, list_ref, at, place):
        total = None
        for b in range(partners):
            row = got_ref[place(list_ref[at, b])]
            rows = jnp.concatenate([row[:, :rank], row[:, rank:]], axis=0)
            part = lax.dot_general(rows, tiles_ref[at, b], NT, preferred_element_type=f32)
            total = part if total is None else total + part
        return total

    def one_parent(parent, carry):
        coarse = field(coarse_ref, coarse_list_ref, parent, lambda r: r * width + 2).astype(bf16)
        for child in range(2):
            leaf = 2 * parent + child
            local = field(fine_ref, fine_list_ref, leaf, lambda r: (r // 2) * width + r % 2)
            local += lax.dot_general(
                coarse, transfer_ref[parent, child], NT, preferred_element_type=f32
            )
            cols = pl.ds(pl.multiple_of(leaf * pts, pts), pts)
            far = jnp.dot(local.astype(bf16), basis_ref[leaf], preferred_element_type=f32)
            value = (near_ref[:, cols] + far).astype(bf16)
            out_ref[:, cols] = value
            for copy in range(copies_ref.shape[0]):
                copies_ref[copy, :, cols] = value
        return carry

    lax.fori_loop(0, leaf_dev // 2, one_parent, 0)


def far_field(
    far_fine, far_coarse, got, coupling_fine, coupling_coarse, transfer, basis, near, copies
):
    vec_dev, points = near.shape
    return pl.pallas_call(
        far_kernel,
        out_shape=(
            jax.ShapeDtypeStruct((vec_dev, points), bf16),
            jax.ShapeDtypeStruct((copies, vec_dev, points), bf16),
        ),
        in_specs=[SM, SM] + [VM] * 6,
        out_specs=(VM, VM),
        compiler_params=params(20),
        name="far_field",
    )(far_fine, far_coarse, got, coupling_fine, coupling_coarse, transfer, basis, near)


def gram_kernel(own_ref, all_ref, out_ref):
    leaf_dev = out_ref.shape[0]
    pts = own_ref.shape[1] // leaf_dev
    for leaf in range(leaf_dev):
        cols = slice(leaf * pts, (leaf + 1) * pts)
        out_ref[leaf] = lax.dot_general(
            own_ref[:, cols], all_ref[:, cols], NT, preferred_element_type=f32
        ) * (1.0 / pts)


def gram(own, rows, leaf_dev):
    return pl.pallas_call(
        gram_kernel,
        out_shape=jax.ShapeDtypeStruct((leaf_dev, own.shape[0], rows.shape[0]), f32),
        in_specs=[VM, VM],
        out_specs=VM,
        compiler_params=params(6),
        name="gram",
    )(own, rows)


def per_device(
    samples,
    coords,
    panel_area,
    quad_weight,
    leaf_basis,
    transfer,
    coupling_fine,
    coupling_coarse,
    near_list,
    send_fine,
    send_coarse,
    far_fine,
    far_coarse,
):
    vec_dev, points = samples.shape
    leaf_dev, rank, pts = leaf_basis.shape
    devices = lax.axis_size("leaf")
    groups = lax.axis_size("vec")
    device = lax.axis_index("leaf")

    own = source_rows(samples, coords, panel_area, quad_weight)
    forward = [(i, i + 1) for i in range(devices - 1)]
    backward = [(i + 1, i) for i in range(devices - 1)]
    low = lax.ppermute(own, "leaf", forward)
    high = lax.ppermute(own, "leaf", backward)

    sent = send_rows(send_fine, send_coarse, samples, leaf_basis, transfer)
    half = sent.shape[1]
    got = lax.all_to_all(
        sent.reshape(devices, -1, LANES), "leaf", split_axis=0, concat_axis=0, tiled=True
    ).reshape(-1, half, LANES)

    first = (device * leaf_dev - HW).astype(jnp.int32).reshape(1)
    near = near_field(first, near_list, coords, own, low, high, pts)
    sample_out, copies = far_field(
        far_fine, far_coarse, got, coupling_fine, coupling_coarse, transfer, leaf_basis, near, groups
    )
    rows = lax.all_to_all(copies, "vec", split_axis=0, concat_axis=0, tiled=True)
    sample_gram = gram(sample_out, rows.reshape(groups * vec_dev, points), leaf_dev)
    return (sample_out, sample_gram)


def solution(mesh):
    return jax.shard_map(
        per_device,
        mesh=mesh,
        in_specs=(
            P("vec", "leaf"),
            P(None, "leaf"),
            P("leaf"),
            P("leaf"),
            P("leaf", None, None),
            P("leaf", None, None, None),
            P("leaf", None, None, None),
            P("leaf", None, None, None),
            P("leaf", None),
            P("leaf", None),
            P("leaf", None),
            P("leaf", None),
            P("leaf", None),
        ),
        out_specs=(P("vec", "leaf"), P("leaf", "vec", None)),
        check_vma=False,
    )
```

time: 214 us -> 128 us (0.60)
  the two profiles are of different devices: /device:TPU:32 before, /device:TPU:64 now
where the time goes in v1:
time: 128 us
  Pallas kernels  41.1 us (32%)
  waiting for transfers between devices  27.5 us (21%)
  starting transfers between devices  26.2 us (20%)
  local copies, waits for them, and re-layouts  19.7 us (15%)
  blocking collectives  12.3 us (10%)
    ppermute x1, waiting for transfers between devices, per_device(): low = lax.ppermute(own, 'leaf', forward)  27.5 us
    pallas_call x1, Pallas kernels, near_field(): pl.pallas_call(near_kernel, out_shape=jax.ShapeDtypeStruct((vec_dev, poin...  27 us
    unnamed x52, local copies, waits for them, and re-layouts  19.7 us
    all_to_all x1, starting transfers between devices, per_device(): lax.all_to_all(sent.reshape(devices, -1, LANES), 'leaf', split_axis=0, co...  18.5 us
    all_to_all x1, blocking collectives, per_device(): lax.all_to_all(copies, 'vec', split_axis=0, concat_axis=0, tiled=True)  12.3 us
    pallas_call x1, Pallas kernels, far_field(): pl.pallas_call(far_kernel, out_shape=(jax.ShapeDtypeStruct((vec_dev, poin...  10.3 us
    ppermute x1, starting transfers between devices, per_device(): high = lax.ppermute(own, 'leaf', backward)  5.61 us
  transfers between devices with their start and end apart: 3, of which 1 were waited for; matrix products, arithmetic and copies ran while one was open for 0% of the time, Pallas kernels for 21%

profile of v1, /device:TPU:64, one launch (start us, length us, event | category | flops | bytes accessed | tf_op | source)
XLA Modules:
  0.0 127.5 jit_solution(16278837345061351943)
XLA Ops:
  0.6 1.0 copy-done.1
  1.7 0.9 copy-done.4
  2.6 0.9 copy-done.6
  4.9 2.5 %send_rows.1 = bf16[384,8,128]{2,1,0:T(8,128)(2,1)} custom-call(s32[2,128]{1,0:T(2,128)S(1)} %bitcast.12, s32[1,128]{1,0:T(1,128)S(1)} %bitcast.13, bf16[16,4096]{1,0:T(8,128)(2,1)S(1)} %copy-done.6, bf16[16,64,256]{2,1,0:T(8,128)(2,1)S(1)} %copy-done.1, bf16[8,2,64,64]{3,2,1,0:T(8,128)(2,1)S(1)} %copy-done.4), custom_call_target="tpu_custom_call" | custom-call | tf_op jit(solution)/shard_map/send_rows/pallas_call | solution.py:119
  7.3 18.5 %all-to-all-start = ((bf16[128,24,128]{2,1,0:T(8,128)(2,1)}), bf16[128,24,128]{2,1,0:T(8,128)(2,1)S(1)}, u32[]{:S(2)}, u32[]{:S(2)}) async-start(bf16[128,24,128]{2,1,0:T(8,128)(2,1)} %bitcast.2), calls=%async_computation | async-start | bytes 1572864 | tf_op jit(solution)/shard_map/all_to_all | solution.py:305
  25.9 0.9 copy-done.7
  26.8 0.8 copy-done.13
  28.4 0.7 copy-done.16
  29.4 2.1 %collective-permute-start = (bf16[32,4096]{1,0:T(8,128)(2,1)S(1)}, bf16[32,4096]{1,0:T(8,128)(2,1)S(1)}, u32[]{:S(2)}, u32[]{:S(2)}) collective-permute-start(bf16[32,4096]{1,0:T(8,128)(2,1)S(1)} %source_rows.1.own_ref), channel_id=1, source_target_pairs={{0,4},{4,8},{8,12},{12,16},{16,20},{20,24},{24,28},{28,32},{32,36}... | collective-permute-start | bytes 786440 | tf_op jit(solution)/shard_map/ppermute | solution.py:300
  31.5 5.6 %collective-permute-start.1 = (bf16[32,4096]{1,0:T(8,128)(2,1)S(1)}, bf16[32,4096]{1,0:T(8,128)(2,1)S(1)}, u32[]{:S(2)}, u32[]{:S(2)}) collective-permute-start(bf16[32,4096]{1,0:T(8,128)(2,1)S(1)} %source_rows.1.own_ref), channel_id=1, source_target_pairs={{4,0},{8,4},{12,8},{16,12},{20,16},{24,20},{28,24},{32,28},{36,32}... | collective-permute-start | bytes 786440 | tf_op jit(solution)/shard_map/ppermute | solution.py:301
  37.9 27.5 %collective-permute-done.low_ref = bf16[32,4096]{1,0:T(8,128)(2,1)S(1)} collective-permute-done((bf16[32,4096]{1,0:T(8,128)(2,1)S(1)}, bf16[32,4096]{1,0:T(8,128)(2,1)S(1)}, u32[]{:S(2)}, u32[]{:S(2)}) %collective-permute-start) | collective-permute-done | bytes 262176 | tf_op jit(solution)/shard_map/ppermute | solution.py:300
  66.8 0.9 copy-done.11
  67.7 0.8 copy-done.14
  68.6 0.9 copy-done.22
  69.5 0.9 copy-done.24
  71.2 27.0 %near_field.1.near_ref = f32[16,4096]{1,0:T(8,128)S(1)} custom-call(s32[1]{0:T(128)} %bitcast.4.first_ref, s32[16,16]{1,0:T(8,128)S(1)} %copy-done.25, f32[3,4096]{1,0:T(4,128)S(1)} %copy-done.14, bf16[32,4096]{1,0:T(8,128)(2,1)S(1)} %copy-done.11, bf16[32,4096]{1,0:T(8,128)(2,1)S(1)} %copy-done.22, bf16[32,4096]{1,0:T(8,128)(2,1)S(1)} %copy-done.24), custom_call_target="tpu_custom_call" | custom-call | flops 17179869184 | bytes 4194304 | tf_op jit(solution)/shard_map/near_field/pallas_call | solution.py:177
  98.2 0.7 copy-done.8
  99.0 2.2 %copy-done = bf16[16,16,64,64]{3,2,1,0:T(8,128)(2,1)S(1)} copy-done((bf16[16,16,64,64]{3,2,1,0:T(8,128)(2,1)S(1)}, bf16[16,16,64,64]{3,2,1,0:T(8,128)(2,1)}, u32[]{:S(2)}) %copy-start) | copy-done | bytes 2097176
  101.2 0.9 copy-done.5
  102.1 0.9 copy-done.9
  103.1 10.3 %far_field.1 = (bf16[16,4096]{1,0:T(8,128)(2,1)}, bf16[4,16,4096]{2,1,0:T(8,128)(2,1)S(1)}) custom-call(s32[16,16]{1,0:T(8,128)S(1)} %copy-done.17, s32[8,16]{1,0:T(8,128)S(1)} %copy-done.18, bf16[384,8,128]{2,1,0:T(8,128)(2,1)S(1)} %bitcast.8, bf16[16,16,64,64]{3,2,1,0:T(8,128)(2,1)S(1)} %copy-done, bf16[8,16,64,64]{3,2,1,0:T(8,128)(2,1)S(1)} %copy-done.3, ...), custom_call_target="tpu_custom_call" | custom-call | tf_op jit(solution)/shard_map/far_field/pallas_call | solution.py:242
  113.4 12.3 %all_to_all.10 = bf16[4,16,4096]{2,1,0:T(8,128)(2,1)S(1)} all-to-all(bf16[4,16,4096]{2,1,0:T(8,128)(2,1)S(1)} %get-tuple-element.5), channel_id=1, replica_groups=mesh['leaf'=128,'vec'=4] {'vec'}, dimensions={0} | all-to-all | bytes 1048576 | tf_op jit(solution)/shard_map/all_to_all | solution.py:314
  125.7 0.9 copy-done.12
  126.6 0.9 gram.1
  (40 shorter events, 5.3 us)
Async XLA Ops:
  0.6 1.0 copy-start.1
  1.7 0.9 copy-start.4
  2.6 0.9 copy-start.6
  7.3 91.6 %all-to-all-start = ((bf16[128,24,128]{2,1,0:T(8,128)(2,1)}), bf16[128,24,128]{2,1,0:T(8,128)(2,1)S(1)}, u32[]{:S(2)}, u32[]{:S(2)}) async-start(bf16[128,24,128]{2,1,0:T(8,128)(2,1)} %bitcast.2), calls=%async_computation | async-start | bytes 1572864 | tf_op jit(solution)/shard_map/all_to_all | solution.py:305
  25.9 0.9 copy-start.7
  26.8 0.8 copy-start.13
  27.6 0.7 copy-start.15
  28.4 0.7 copy-start.16
  29.4 35.9 %collective-permute-start = (bf16[32,4096]{1,0:T(8,128)(2,1)S(1)}, bf16[32,4096]{1,0:T(8,128)(2,1)S(1)}, u32[]{:S(2)}, u32[]{:S(2)}) collective-permute-start(bf16[32,4096]{1,0:T(8,128)(2,1)S(1)} %source_rows.1.own_ref), channel_id=1, source_target_pairs={{0,4},{4,8},{8,12},{12,16},{16,20},{20,24},{24,28},{28,32},{32,36}... | collective-permute-start | bytes 786440 | tf_op jit(solution)/shard_map/ppermute | solution.py:300
  31.5 34.6 %collective-permute-start.1 = (bf16[32,4096]{1,0:T(8,128)(2,1)S(1)}, bf16[32,4096]{1,0:T(8,128)(2,1)S(1)}, u32[]{:S(2)}, u32[]{:S(2)}) collective-permute-start(bf16[32,4096]{1,0:T(8,128)(2,1)S(1)} %source_rows.1.own_ref), channel_id=1, source_target_pairs={{4,0},{8,4},{12,8},{16,12},{20,16},{24,20},{28,24},{32,28},{36,32}... | collective-permute-start | bytes 786440 | tf_op jit(solution)/shard_map/ppermute | solution.py:301
  37.1 0.7 copy-start.10
  66.8 0.9 copy-start.11
  67.7 0.8 copy-start.14
  68.6 0.9 copy-start.22
  69.5 0.9 copy-start.24
  71.2 27.8 %copy-start.2 = (bf16[16,64,256]{2,1,0:T(8,128)(2,1)S(1)}, bf16[16,64,256]{2,1,0:T(8,128)(2,1)}, u32[]{:S(2)}) copy-start(bf16[16,64,256]{2,1,0:T(8,128)(2,1)} %basis_ref.3) | copy-start | bytes 1572868
  71.2 27.8 %copy-start.3 = (bf16[8,16,64,64]{3,2,1,0:T(8,128)(2,1)S(1)}, bf16[8,16,64,64]{3,2,1,0:T(8,128)(2,1)}, u32[]{:S(2)}) copy-start(bf16[8,16,64,64]{3,2,1,0:T(8,128)(2,1)} %coarse_ref.1) | copy-start | bytes 3145732
  71.2 27.8 %copy-start.17 = (s32[16,16]{1,0:T(8,128)S(1)}, s32[16,16]{1,0:T(8,128)}, u32[]{:S(2)}) copy-start(s32[16,16]{1,0:T(8,128)} %fine_list_ref.1) | copy-start | bytes 3076
  71.2 27.8 %copy-start.18 = (s32[8,16]{1,0:T(8,128)S(1)}, s32[8,16]{1,0:T(8,128)}, u32[]{:S(2)}) copy-start(s32[8,16]{1,0:T(8,128)} %coarse_list_ref.1) | copy-start | bytes 1540
  98.2 0.7 copy-start.8
  99.0 2.2 %copy-start = (bf16[16,16,64,64]{3,2,1,0:T(8,128)(2,1)S(1)}, bf16[16,16,64,64]{3,2,1,0:T(8,128)(2,1)}, u32[]{:S(2)}) copy-start(bf16[16,16,64,64]{3,2,1,0:T(8,128)(2,1)} %fine_ref.1) | copy-start | bytes 6291460
  101.2 0.9 copy-start.5
  102.1 0.9 copy-start.9
  125.7 0.9 copy-start.12
  (5 other events, 3.5 us)

commit v2 on v1

--- a/solution.py
+++ b/solution.py
@@ -15,12 +15,25 @@
 f32 = jnp.float32
 VM = pl.BlockSpec(memory_space=pltpu.VMEM)
 SM = pl.BlockSpec(memory_space=pltpu.SMEM)
+HB = pl.BlockSpec(memory_space=pltpu.HBM)
 NT = (((1,), (1,)), ((), ()))
 TN = (((0,), (0,)), ((), ()))
 
 
 def params(mebibytes):
     return pltpu.CompilerParams(vmem_limit_bytes=mebibytes << 20)
+
+
+def start_all(pairs, sems):
+    copies = [pltpu.make_async_copy(a, b, sems.at[n]) for n, (a, b) in enumerate(pairs)]
+    for copy in copies:
+        copy.start()
+    return copies
+
+
+def wait_all(copies):
+    for copy in copies:
+        copy.wait()
 
 
 def split3(x):
@@ -49,9 +62,18 @@
     return found.astype(bf16)
 
 
-def source_kernel(samples_ref, coords_ref, area_ref, weight_ref, out_ref):
-    vec_dev = samples_ref.shape[0]
-    out_ref[0:vec_dev, :] = samples_ref[...]
+def source_kernel(samples_hbm, coords_hbm, area_hbm, weight_hbm, out_hbm, rows_v, coords_ref, area_ref, weight_ref, sems):
+    vec_dev = samples_hbm.shape[0]
+    copies = start_all(
+        [
+            (coords_hbm, coords_ref),
+            (area_hbm, area_ref),
+            (weight_hbm, weight_ref),
+            (samples_hbm, rows_v.at[0:vec_dev]),
+        ],
+        sems,
+    )
+    wait_all(copies[:3])
     x, y, z = coords_ref[0:1, :], coords_ref[1:2, :], coords_ref[2:3, :]
     weight = weight_ref[...]
     scale = (16.0 * 3.141592653589793**2) / (weight * weight)
@@ -60,30 +82,65 @@
     for axis in (x, y, z):
         rows += split3(-2.0 * scale * axis)
     rows.append(jnp.zeros_like(scale))
-    out_ref[vec_dev:, :] = jnp.concatenate(rows, axis=0).astype(bf16)
+    rows_v[vec_dev:, :] = jnp.concatenate(rows, axis=0).astype(bf16)
+    copies[3].wait()
+    wait_all(start_all([(rows_v, out_hbm)], sems))
 
 
 def source_rows(samples, coords, panel_area, quad_weight):
     vec_dev, points = samples.shape
+    shape = (vec_dev + FEATURES, points)
     return pl.pallas_call(
         source_kernel,
-        out_shape=jax.ShapeDtypeStruct((vec_dev + FEATURES, points), bf16),
-        in_specs=[VM] * 4,
-        out_specs=VM,
-        compiler_params=params(6),
+        out_shape=jax.ShapeDtypeStruct(shape, bf16),
+        in_specs=[HB] * 4,
+        out_specs=HB,
+        scratch_shapes=[
+            pltpu.VMEM(shape, bf16),
+            pltpu.VMEM(coords.shape, f32),
+            pltpu.VMEM((1, points), f32),
+            pltpu.VMEM((1, points), f32),
+            pltpu.SemaphoreType.DMA((4,)),
+        ],
+        compiler_params=params(60),
         name="source_rows",
     )(samples, coords, panel_area.reshape(1, -1), quad_weight.reshape(1, -1))
 
 
-def coef_kernel(fine_ref, coarse_ref, samples_ref, basis_ref, transfer_ref, out_ref, table):
+def coef_kernel(
+    fine_hbm,
+    coarse_hbm,
+    own_hbm,
+    basis_hbm,
+    transfer_hbm,
+    out_ref,
+    table,
+    fine_ref,
+    coarse_ref,
+    samples_ref,
+    basis_ref,
+    transfer_ref,
+    sems,
+):
     leaf_dev, rank, pts = basis_ref.shape
     half = samples_ref.shape[0] // 2
     devices = fine_ref.shape[1]
+    copies = start_all(
+        [
+            (own_hbm.at[0 : 2 * half], samples_ref),
+            (basis_hbm, basis_ref),
+            (transfer_hbm, transfer_ref),
+            (fine_hbm, fine_ref),
+            (coarse_hbm, coarse_ref),
+        ],
+        sems,
+    )
     fine = []
 
     def keep(at, value):
         table[at] = jnp.concatenate([value[:half], value[half:]], axis=1).astype(bf16)
 
+    wait_all(copies[:2])
     for leaf in range(leaf_dev):
         value = lax.dot_general(
             samples_ref[:, leaf * pts : (leaf + 1) * pts],
@@ -93,11 +150,13 @@
         )
         keep(leaf, value)
         fine.append(value.astype(bf16))
+    copies[2].wait()
     for parent in range(leaf_dev // 2):
         value = jnp.dot(fine[2 * parent], transfer_ref[parent, 0], preferred_element_type=f32)
         value += jnp.dot(fine[2 * parent + 1], transfer_ref[parent, 1], preferred_element_type=f32)
         keep(leaf_dev + parent, value)
 
+    wait_all(copies[3:])
     slots, parents = fine_ref.shape[0], coarse_ref.shape[0]
     width = slots + parents
 
@@ -111,26 +170,62 @@
     lax.fori_loop(0, devices, fill, 0, unroll=8)
 
 
-def send_rows(send_fine, send_coarse, samples, leaf_basis, transfer):
-    leaf_dev, rank, _ = leaf_basis.shape
-    half = samples.shape[0] // 2
+def send_rows(send_fine, send_coarse, own, leaf_basis, transfer):
+    leaf_dev, rank, pts = leaf_basis.shape
+    vec_dev = own.shape[0] - FEATURES
+    half = vec_dev // 2
     devices = send_fine.shape[0]
     width = send_fine.shape[1] + send_coarse.shape[1]
     return pl.pallas_call(
         coef_kernel,
         out_shape=jax.ShapeDtypeStruct((devices * width, half, 2 * rank), bf16),
-        in_specs=[SM, SM] + [VM] * 3,
+        in_specs=[HB] * 5,
         out_specs=VM,
-        scratch_shapes=[pltpu.VMEM((leaf_dev + leaf_dev // 2, half, 2 * rank), bf16)],
-        compiler_params=params(8),
+        scratch_shapes=[
+            pltpu.VMEM((leaf_dev + leaf_dev // 2, half, 2 * rank), bf16),
+            pltpu.SMEM(send_fine.shape[::-1], jnp.int32),
+            pltpu.SMEM(send_coarse.shape[::-1], jnp.int32),
+            pltpu.VMEM((vec_dev, own.shape[1]), bf16),
+            pltpu.VMEM(leaf_basis.shape, bf16),
+            pltpu.VMEM(transfer.shape, bf16),
+            pltpu.SemaphoreType.DMA((5,)),
+        ],
+        compiler_params=params(60),
         name="send_rows",
-    )(send_fine.T, send_coarse.T, samples, leaf_basis, transfer)
-
-
-def near_kernel(first_ref, list_ref, coords_ref, own_ref, low_ref, high_ref, out_ref, feat, vals):
+    )(send_fine.T, send_coarse.T, own, leaf_basis, transfer)
+
+
+def near_kernel(
+    first_ref,
+    list_hbm,
+    coords_hbm,
+    own_hbm,
+    low_hbm,
+    high_hbm,
+    out_hbm,
+    feat,
+    vals,
+    list_ref,
+    coords_ref,
+    own_ref,
+    low_ref,
+    high_ref,
+    out_ref,
+    sems,
+):
     vec_dev = out_ref.shape[0]
     leaf_dev, partners = list_ref.shape
     pts = feat.shape[2]
+    copies = start_all(
+        [
+            (own_hbm, own_ref),
+            (low_hbm, low_ref),
+            (high_hbm, high_ref),
+            (list_hbm, list_ref),
+            (coords_hbm, coords_ref),
+        ],
+        sems,
+    )
     target_rows, source_rows_ = term_rows()
     wide = selection(
         source_rows_,
@@ -142,6 +237,7 @@
         lax.broadcasted_iota(jnp.int32, (FEATURES, TERMS), 1),
         lax.broadcasted_iota(jnp.int32, (FEATURES, TERMS), 0),
     )
+    wait_all(copies)
     for place, part in enumerate((low_ref, own_ref, high_ref)):
         for leaf in range(leaf_dev):
             cols = slice(leaf * pts, (leaf + 1) * pts)
@@ -167,6 +263,7 @@
         return carry
 
     lax.fori_loop(0, leaf_dev, one_leaf, 0)
+    wait_all(start_all([(out_ref, out_hbm)], sems))
 
 
 def near_field(first, near_list, coords, own, low, high, pts):
@@ -177,13 +274,20 @@
     return pl.pallas_call(
         near_kernel,
         out_shape=jax.ShapeDtypeStruct((vec_dev, points), f32),
-        in_specs=[SM, SM] + [VM] * 4,
-        out_specs=VM,
+        in_specs=[SM] + [HB] * 5,
+        out_specs=HB,
         scratch_shapes=[
             pltpu.VMEM((3 * leaf_dev, TERMS, pts), bf16),
             pltpu.VMEM((3 * leaf_dev, vec_dev, pts), bf16),
-        ],
-        compiler_params=params(8),
+            pltpu.SMEM(near_list.shape, jnp.int32),
+            pltpu.VMEM(coords.shape, f32),
+            pltpu.VMEM(own.shape, bf16),
+            pltpu.VMEM(own.shape, bf16),
+            pltpu.VMEM(own.shape, bf16),
+            pltpu.VMEM((vec_dev, points), f32),
+            pltpu.SemaphoreType.DMA((5,)),
+        ],
+        compiler_params=params(60),
         cost_estimate=pl.CostEstimate(
             flops=2 * 512 * pairs, transcendentals=pairs, bytes_accessed=4 << 20
         ),
@@ -192,6 +296,16 @@
 
 
 def far_kernel(
+    fine_list_hbm,
+    coarse_list_hbm,
+    got_hbm,
+    fine_hbm,
+    coarse_hbm,
+    transfer_hbm,
+    basis_hbm,
+    near_hbm,
+    out_ref,
+    copies_ref,
     fine_list_ref,
     coarse_list_ref,
     got_ref,
@@ -200,27 +314,68 @@
     transfer_ref,
     basis_ref,
     near_ref,
-    out_ref,
-    copies_ref,
+    sems,
+    fine_sems,
+    coarse_sems,
 ):
     leaf_dev, partners = fine_list_ref.shape
     width = 3
     rank, pts = basis_ref.shape[1:]
+    half = got_ref.shape[1]
+    copies = start_all(
+        [
+            (coarse_list_hbm, coarse_list_ref),
+            (fine_list_hbm, fine_list_ref),
+            (got_hbm, got_ref),
+            (transfer_hbm, transfer_ref),
+            (basis_hbm, basis_ref),
+            (near_hbm, near_ref),
+        ],
+        sems,
+    )
+
+    def blocks(parent):
+        two = pl.ds(2 * parent, 2)
+        return (
+            pltpu.make_async_copy(
+                coarse_hbm.at[parent], coarse_ref.at[parent], coarse_sems.at[parent]
+            ),
+            pltpu.make_async_copy(fine_hbm.at[two], fine_ref.at[two], fine_sems.at[parent]),
+        )
+
+    for parent in range(leaf_dev // 2):
+        for copy in blocks(parent):
+            copy.start()
+    wait_all(copies)
+    left = lax.broadcasted_iota(jnp.int32, (half, 2 * rank), 1) < rank
+
+    def joined(first, second):
+        first, second = first.astype(f32), second.astype(f32)
+        return jnp.concatenate(
+            [
+                jnp.where(left, first, pltpu.roll(second, rank, 1)),
+                jnp.where(left, pltpu.roll(first, rank, 1), second),
+            ],
+            axis=0,
+        ).astype(bf16)
 
     def field(tiles_ref, list_ref, at, place):
         total = None
-        for b in range(partners):
-            row = got_ref[place(list_ref[at, b])]
-            rows = jnp.concatenate([row[:, :rank], row[:, rank:]], axis=0)
-            part = lax.dot_general(rows, tiles_ref[at, b], NT, preferred_element_type=f32)
+        for b in range(0, partners, 4):
+            rows = [got_ref[place(list_ref[at, b + n])] for n in range(4)]
+            rows = jnp.concatenate([joined(*rows[:2]), joined(*rows[2:])], axis=1)
+            tiles = jnp.concatenate([tiles_ref[at, b + n] for n in range(4)], axis=1)
+            part = lax.dot_general(rows, tiles, NT, preferred_element_type=f32)
             total = part if total is None else total + part
         return total
 
     def one_parent(parent, carry):
+        for copy in blocks(parent):
+            copy.wait()
         coarse = field(coarse_ref, coarse_list_ref, parent, lambda r: r * width + 2).astype(bf16)
         for child in range(2):
             leaf = 2 * parent + child
-            local = field(fine_ref, fine_list_ref, leaf, lambda r: (r // 2) * width + r % 2)
+            local = field(fine_ref, fine_list_ref, leaf, lambda r: (r >> 1) * width + (r & 1))
             local += lax.dot_general(
                 coarse, transfer_ref[parent, child], NT, preferred_element_type=f32
             )
@@ -239,38 +394,49 @@
     far_fine, far_coarse, got, coupling_fine, coupling_coarse, transfer, basis, near, copies
 ):
     vec_dev, points = near.shape
+    held = (got, coupling_fine, coupling_coarse, transfer, basis, near)
+    parents = coupling_coarse.shape[0]
     return pl.pallas_call(
         far_kernel,
         out_shape=(
             jax.ShapeDtypeStruct((vec_dev, points), bf16),
             jax.ShapeDtypeStruct((copies, vec_dev, points), bf16),
         ),
-        in_specs=[SM, SM] + [VM] * 6,
+        in_specs=[HB] * 8,
         out_specs=(VM, VM),
-        compiler_params=params(20),
+        scratch_shapes=[
+            pltpu.SMEM(far_fine.shape, jnp.int32),
+            pltpu.SMEM(far_coarse.shape, jnp.int32),
+            *[pltpu.VMEM(a.shape, a.dtype) for a in held],
+            pltpu.SemaphoreType.DMA((6,)),
+            pltpu.SemaphoreType.DMA((parents,)),
+            pltpu.SemaphoreType.DMA((parents,)),
+        ],
+        compiler_params=params(60),
         name="far_field",
-    )(far_fine, far_coarse, got, coupling_fine, coupling_coarse, transfer, basis, near)
-
-
-def gram_kernel(own_ref, all_ref, out_ref):
-    leaf_dev = out_ref.shape[0]
-    pts = own_ref.shape[1] // leaf_dev
+    )(far_fine, far_coarse, *held)
+
+
+def gram_kernel(me_ref, all_ref, out_ref):
+    leaf_dev, vec_dev = out_ref.shape[:2]
+    pts = all_ref.shape[1] // leaf_dev
+    mine = pl.ds(pl.multiple_of(me_ref[0] * vec_dev, vec_dev), vec_dev)
     for leaf in range(leaf_dev):
         cols = slice(leaf * pts, (leaf + 1) * pts)
         out_ref[leaf] = lax.dot_general(
-            own_ref[:, cols], all_ref[:, cols], NT, preferred_element_type=f32
+            all_ref[mine, cols], all_ref[:, cols], NT, preferred_element_type=f32
         ) * (1.0 / pts)
 
 
-def gram(own, rows, leaf_dev):
+def gram(me, rows, vec_dev, leaf_dev):
     return pl.pallas_call(
         gram_kernel,
-        out_shape=jax.ShapeDtypeStruct((leaf_dev, own.shape[0], rows.shape[0]), f32),
-        in_specs=[VM, VM],
+        out_shape=jax.ShapeDtypeStruct((leaf_dev, vec_dev, rows.shape[0]), f32),
+        in_specs=[SM, VM],
         out_specs=VM,
         compiler_params=params(6),
         name="gram",
-    )(own, rows)
+    )(me, rows)
 
 
 def per_device(
@@ -300,8 +466,9 @@
     low = lax.ppermute(own, "leaf", forward)
     high = lax.ppermute(own, "leaf", backward)
 
-    sent = send_rows(send_fine, send_coarse, samples, leaf_basis, transfer)
+    sent = send_rows(send_fine, send_coarse, own, leaf_basis, transfer)
     half = sent.shape[1]
+    sent, low, high = lax.optimization_barrier((sent, low, high))
     got = lax.all_to_all(
         sent.reshape(devices, -1, LANES), "leaf", split_axis=0, concat_axis=0, tiled=True
     ).reshape(-1, half, LANES)
@@ -312,7 +479,8 @@
         far_fine, far_coarse, got, coupling_fine, coupling_coarse, transfer, leaf_basis, near, groups
     )
     rows = lax.all_to_all(copies, "vec", split_axis=0, concat_axis=0, tiled=True)
-    sample_gram = gram(sample_out, rows.reshape(groups * vec_dev, points), leaf_dev)
+    me = lax.axis_index("vec").astype(jnp.int32).reshape(1)
+    sample_gram = gram(me, rows.reshape(groups * vec_dev, points), vec_dev, leaf_dev)
     return (sample_out, sample_gram)
 
 

time: 128 us -> 104 us (0.81)
  the two profiles are of different devices: /device:TPU:64 before, /device:TPU:32 now
where the time goes in v2:
time: 104 us
  Pallas kernels  43.7 us (42%)
  waiting for transfers between devices  31 us (30%)
  starting transfers between devices  27.8 us (27%)
    pallas_call x1, Pallas kernels, near_field(): pl.pallas_call(near_kernel, out_shape=jax.ShapeDtypeStruct((vec_dev, poin...  28.2 us
    all_to_all x1, starting transfers between devices, per_device(): lax.all_to_all(sent.reshape(devices, -1, LANES), 'leaf', split_axis=0, co...  17.8 us
    all_to_all x1, waiting for transfers between devices, per_device(): lax.all_to_all(sent.reshape(devices, -1, LANES), 'leaf', split_axis=0, co...  16 us
    all_to_all x1, waiting for transfers between devices, per_device(): lax.all_to_all(copies, 'vec', split_axis=0, concat_axis=0, tiled=True)  10.2 us
    pallas_call x1, Pallas kernels, far_field(): pl.pallas_call(far_kernel, out_shape=(jax.ShapeDtypeStruct((vec_dev, poin...  9.46 us
    ppermute x1, waiting for transfers between devices, per_device(): low = lax.ppermute(own, 'leaf', forward)  4.83 us
    all_to_all x1, starting transfers between devices, per_device(): lax.all_to_all(copies, 'vec', split_axis=0, concat_axis=0, tiled=True)  4.48 us
    ppermute x1, starting transfers between devices, per_device(): high = lax.ppermute(own, 'leaf', backward)  3.65 us
  transfers between devices with their start and end apart: 4, of which 3 were waited for; matrix products, arithmetic and copies ran while one was open for 0% of the time, Pallas kernels for 30%

profile of v2, /device:TPU:32, one launch (start us, length us, event | category | flops | bytes accessed | tf_op | source)
XLA Modules:
  0.0 104.1 jit_solution(14534147888480481236)
XLA Ops:
  0.6 1.9 %source_rows.1.own_hbm = bf16[32,4096]{1,0:T(8,128)(2,1)} custom-call(bf16[16,4096]{1,0:T(8,128)(2,1)} %samples_hbm.1, f32[3,4096]{1,0:T(4,128)} %coords_hbm.3, f32[1,4096]{1,0:T(1,128)} %bitcast.12, f32[1,4096]{1,0:T(1,128)} %bitcast.13), custom_call_target="tpu_custom_call" | custom-call | tf_op jit(solution)/shard_map/source_rows/pallas_call | solution.py:93
  2.6 3.7 %collective-permute-start.1 = (bf16[32,4096]{1,0:T(8,128)(2,1)}, bf16[32,4096]{1,0:T(8,128)(2,1)S(1)}, u32[]{:S(2)}, u32[]{:S(2)}) collective-permute-start(bf16[32,4096]{1,0:T(8,128)(2,1)} %source_rows.1.own_hbm), channel_id=1, source_target_pairs={{4,0},{8,4},{12,8},{16,12},{20,16},{24,20},{28,24},{32,28},{36,32}... | collective-permute-start | bytes 786440 | tf_op jit(solution)/shard_map/ppermute | solution.py:467
  6.2 1.9 %collective-permute-start = (bf16[32,4096]{1,0:T(8,128)(2,1)}, bf16[32,4096]{1,0:T(8,128)(2,1)S(1)}, u32[]{:S(2)}, u32[]{:S(2)}) collective-permute-start(bf16[32,4096]{1,0:T(8,128)(2,1)} %source_rows.1.own_hbm), channel_id=1, source_target_pairs={{0,4},{4,8},{8,12},{12,16},{16,20},{20,24},{24,28},{28,32},{32,36}... | collective-permute-start | bytes 786440 | tf_op jit(solution)/shard_map/ppermute | solution.py:466
  8.2 3.2 %send_rows.1 = bf16[384,8,128]{2,1,0:T(8,128)(2,1)} custom-call(s32[2,128]{1,0:T(2,128)} %bitcast.14, s32[1,128]{1,0:T(1,128)} %bitcast.15, bf16[32,4096]{1,0:T(8,128)(2,1)} %source_rows.1.own_hbm, bf16[16,64,256]{2,1,0:T(8,128)(2,1)} %basis_hbm.3, bf16[8,2,64,64]{3,2,1,0:T(8,128)(2,1)} %transfer_hbm.3), custom_call_target="tpu_custom_call" | custom-call | tf_op jit(solution)/shard_map/send_rows/pallas_call | solution.py:179
  11.4 0.0 collective-permute-done.1.high_hbm
  11.4 0.0 copy-start.1
  11.4 4.8 %collective-permute-done.low_hbm = bf16[32,4096]{1,0:T(8,128)(2,1)S(1)} collective-permute-done((bf16[32,4096]{1,0:T(8,128)(2,1)}, bf16[32,4096]{1,0:T(8,128)(2,1)S(1)}, u32[]{:S(2)}, u32[]{:S(2)}) %collective-permute-start) | collective-permute-done | bytes 262176 | tf_op jit(solution)/shard_map/ppermute | solution.py:466
  16.2 0.0 copy-start.2
  16.2 17.8 %all-to-all-start = ((bf16[128,24,128]{2,1,0:T(8,128)(2,1)}), bf16[128,24,128]{2,1,0:T(8,128)(2,1)S(1)}, u32[]{:S(2)}, u32[]{:S(2)}) async-start(bf16[128,24,128]{2,1,0:T(8,128)(2,1)} %bitcast.11), calls=%async_computation | async-start | bytes 1572864 | tf_op jit(solution)/shard_map/all_to_all | solution.py:472
  34.0 0.0 copy-done.1
  34.0 0.0 copy-done.2
  34.0 28.2 %near_field.1.near_hbm = f32[16,4096]{1,0:T(8,128)} custom-call(s32[1]{0:T(128)} %bitcast.6.first_ref, s32[16,16]{1,0:T(8,128)} %list_hbm.1, f32[3,4096]{1,0:T(4,128)} %coords_hbm.3, bf16[32,4096]{1,0:T(8,128)(2,1)} %source_rows.1.own_hbm, bf16[32,4096]{1,0:T(8,128)(2,1)} %copy-done.2, bf16[32,4096]{1,0:T(8,128)(2,1)} %copy-done.1), custom_call_target="tpu_custom_call" | custom-call | flops 17179869184 | bytes 4194304 | tf_op jit(solution)/shard_map/near_field/pallas_call | solution.py:274
  62.2 16.0 %all-to-all-done = bf16[128,24,128]{2,1,0:T(8,128)(2,1)S(1)} async-done(((bf16[128,24,128]{2,1,0:T(8,128)(2,1)}), bf16[128,24,128]{2,1,0:T(8,128)(2,1)S(1)}, u32[]{:S(2)}, u32[]{:S(2)}) %all-to-all-start) | async-done | bytes 786464 | tf_op jit(solution)/shard_map/all_to_all | solution.py:472
  78.2 0.0 copy-start
  78.2 0.9 copy-done
  79.1 9.5 %far_field.1 = (bf16[16,4096]{1,0:T(8,128)(2,1)}, bf16[4,16,4096]{2,1,0:T(8,128)(2,1)}) custom-call(s32[16,16]{1,0:T(8,128)} %fine_list_hbm.1, s32[8,16]{1,0:T(8,128)} %coarse_list_hbm.1, bf16[384,8,128]{2,1,0:T(8,128)(2,1)} %bitcast.10, bf16[16,16,64,64]{3,2,1,0:T(8,128)(2,1)} %fine_hbm.1, bf16[8,16,64,64]{3,2,1,0:T(8,128)(2,1)} %coarse_hbm.1, ...), custom_call_target="tpu_custom_call" | custom-call | tf_op jit(solution)/shard_map/far_field/pallas_call | solution.py:399
  88.6 4.5 %all-to-all-start.1 = ((bf16[4,16,4096]{2,1,0:T(8,128)(2,1)}), bf16[4,16,4096]{2,1,0:T(8,128)(2,1)S(1)}, u32[]{:S(2)}, u32[]{:S(2)}) async-start(bf16[4,16,4096]{2,1,0:T(8,128)(2,1)} %get-tuple-element.11), calls=%async_computation.1 | async-start | bytes 1048576 | tf_op jit(solution)/shard_map/all_to_all | solution.py:481
  93.0 10.2 %all-to-all-done.1 = bf16[4,16,4096]{2,1,0:T(8,128)(2,1)S(1)} async-done(((bf16[4,16,4096]{2,1,0:T(8,128)(2,1)}), bf16[4,16,4096]{2,1,0:T(8,128)(2,1)S(1)}, u32[]{:S(2)}, u32[]{:S(2)}) %all-to-all-start.1) | async-done | bytes 524320 | tf_op jit(solution)/shard_map/all_to_all | solution.py:481
  103.2 0.9 gram.1
Async XLA Ops:
  2.6 8.8 %collective-permute-start.1 = (bf16[32,4096]{1,0:T(8,128)(2,1)}, bf16[32,4096]{1,0:T(8,128)(2,1)S(1)}, u32[]{:S(2)}, u32[]{:S(2)}) collective-permute-start(bf16[32,4096]{1,0:T(8,128)(2,1)} %source_rows.1.own_hbm), channel_id=1, source_target_pairs={{4,0},{8,4},{12,8},{16,12},{20,16},{24,20},{28,24},{32,28},{36,32}... | collective-permute-start | bytes 786440 | tf_op jit(solution)/shard_map/ppermute | solution.py:467
  6.2 10.0 %collective-permute-start = (bf16[32,4096]{1,0:T(8,128)(2,1)}, bf16[32,4096]{1,0:T(8,128)(2,1)S(1)}, u32[]{:S(2)}, u32[]{:S(2)}) collective-permute-start(bf16[32,4096]{1,0:T(8,128)(2,1)} %source_rows.1.own_hbm), channel_id=1, source_target_pairs={{0,4},{4,8},{8,12},{12,16},{16,20},{20,24},{24,28},{28,32},{32,36}... | collective-permute-start | bytes 786440 | tf_op jit(solution)/shard_map/ppermute | solution.py:466
  11.4 22.6 %copy-start.1 = (bf16[32,4096]{1,0:T(8,128)(2,1)}, bf16[32,4096]{1,0:T(8,128)(2,1)S(1)}, u32[]{:S(2)}) copy-start(bf16[32,4096]{1,0:T(8,128)(2,1)S(1)} %collective-permute-done.1.high_hbm) | copy-start | bytes 786436
  16.2 17.8 %copy-start.2 = (bf16[32,4096]{1,0:T(8,128)(2,1)}, bf16[32,4096]{1,0:T(8,128)(2,1)S(1)}, u32[]{:S(2)}) copy-start(bf16[32,4096]{1,0:T(8,128)(2,1)S(1)} %collective-permute-done.low_hbm) | copy-start | bytes 786436
  16.2 62.0 %all-to-all-start = ((bf16[128,24,128]{2,1,0:T(8,128)(2,1)}), bf16[128,24,128]{2,1,0:T(8,128)(2,1)S(1)}, u32[]{:S(2)}, u32[]{:S(2)}) async-start(bf16[128,24,128]{2,1,0:T(8,128)(2,1)} %bitcast.11), calls=%async_computation | async-start | bytes 1572864 | tf_op jit(solution)/shard_map/all_to_all | solution.py:472
  78.2 0.9 copy-start
  88.6 14.6 %all-to-all-start.1 = ((bf16[4,16,4096]{2,1,0:T(8,128)(2,1)}), bf16[4,16,4096]{2,1,0:T(8,128)(2,1)S(1)}, u32[]{:S(2)}, u32[]{:S(2)}) async-start(bf16[4,16,4096]{2,1,0:T(8,128)(2,1)} %get-tuple-element.11), calls=%async_computation.1 | async-start | bytes 1048576 | tf_op jit(solution)/shard_map/all_to_all | solution.py:481

commit v3 on v2

--- a/solution.py
+++ b/solution.py
@@ -346,7 +346,7 @@
     for parent in range(leaf_dev // 2):
         for copy in blocks(parent):
             copy.start()
-    wait_all(copies)
+    wait_all(copies[:3])
     left = lax.broadcasted_iota(jnp.int32, (half, 2 * rank), 1) < rank
 
     def joined(first, second):
@@ -369,25 +369,32 @@
             total = part if total is None else total + part
         return total
 
-    def one_parent(parent, carry):
-        for copy in blocks(parent):
-            copy.wait()
-        coarse = field(coarse_ref, coarse_list_ref, parent, lambda r: r * width + 2).astype(bf16)
-        for child in range(2):
-            leaf = 2 * parent + child
-            local = field(fine_ref, fine_list_ref, leaf, lambda r: (r >> 1) * width + (r & 1))
-            local += lax.dot_general(
-                coarse, transfer_ref[parent, child], NT, preferred_element_type=f32
+    parents = range(leaf_dev // 2)
+    coarse, local = [], []
+    for first in range(0, leaf_dev // 2, 2):
+        group = range(first, first + 2)
+        for parent in group:
+            for copy in blocks(parent):
+                copy.wait()
+        for parent in group:
+            coarse.append(
+                field(coarse_ref, coarse_list_ref, parent, lambda r: r * width + 2).astype(bf16)
             )
-            cols = pl.ds(pl.multiple_of(leaf * pts, pts), pts)
-            far = jnp.dot(local.astype(bf16), basis_ref[leaf], preferred_element_type=f32)
-            value = (near_ref[:, cols] + far).astype(bf16)
-            out_ref[:, cols] = value
-            for copy in range(copies_ref.shape[0]):
-                copies_ref[copy, :, cols] = value
-        return carry
-
-    lax.fori_loop(0, leaf_dev // 2, one_parent, 0)
+        for leaf in range(2 * first, 2 * first + 2 * 2):
+            local.append(field(fine_ref, fine_list_ref, leaf, lambda r: (r >> 1) * width + (r & 1)))
+    wait_all(copies[3:])
+    for leaf in range(leaf_dev):
+        parent, child = leaf // 2, leaf % 2
+        local[leaf] += lax.dot_general(
+            coarse[parent], transfer_ref[parent, child], NT, preferred_element_type=f32
+        )
+    for leaf in range(leaf_dev):
+        cols = slice(leaf * pts, (leaf + 1) * pts)
+        far = jnp.dot(local[leaf].astype(bf16), basis_ref[leaf], preferred_element_type=f32)
+        value = (near_ref[:, cols] + far).astype(bf16)
+        out_ref[:, cols] = value
+        for copy in range(copies_ref.shape[0]):
+            copies_ref[copy, :, cols] = value
 
 
 def far_field(

time: 104 us -> 100 us (0.962)
  Pallas kernels: 43.7 us -> 39.3 us
    pallas_call x1, Pallas kernels: 9.46 us -> 5.05 us  [far_field(): pl.pallas_call(far_kernel, out_shape=(jax.ShapeDtypeStruct((vec_dev, poin...]
  transfers between devices with their start and end apart: 4 -> 4, of which waited for: 3 -> 3; matrix products, arithmetic and copies ran while one was open for 0% -> 0% of each run, Pallas kernels for 30% -> 32%
where the time goes in v3:
time: 100 us; the launch traced here: 99.7 us
  Pallas kernels  39.3 us (39%)
  waiting for transfers between devices  31 us (31%)
  starting transfers between devices  27.8 us (28%)
    pallas_call x1, Pallas kernels, near_field(): pl.pallas_call(near_kernel, out_shape=jax.ShapeDtypeStruct((vec_dev, poin...  28.2 us
    all_to_all x1, starting transfers between devices, per_device(): lax.all_to_all(sent.reshape(devices, -1, LANES), 'leaf', split_axis=0, co...  17.8 us
    all_to_all x1, waiting for transfers between devices, per_device(): lax.all_to_all(sent.reshape(devices, -1, LANES), 'leaf', split_axis=0, co...  16 us
    all_to_all x1, waiting for transfers between devices, per_device(): lax.all_to_all(copies, 'vec', split_axis=0, concat_axis=0, tiled=True)  10.2 us
    pallas_call x1, Pallas kernels, far_field(): pl.pallas_call(far_kernel, out_shape=(jax.ShapeDtypeStruct((vec_dev, poin...  5.05 us
    ppermute x1, waiting for transfers between devices, per_device(): low = lax.ppermute(own, 'leaf', forward)  4.83 us
    all_to_all x1, starting transfers between devices, per_device(): lax.all_to_all(copies, 'vec', split_axis=0, concat_axis=0, tiled=True)  4.48 us
    ppermute x1, starting transfers between devices, per_device(): high = lax.ppermute(own, 'leaf', backward)  3.65 us
  transfers between devices with their start and end apart: 4, of which 3 were waited for; matrix products, arithmetic and copies ran while one was open for 0% of the time, Pallas kernels for 32%

profile of v3, /device:TPU:32, one launch (start us, length us, event | category | flops | bytes accessed | tf_op | source)
XLA Modules:
  0.0 99.7 jit_solution(10392821127411975238)
XLA Ops:
  0.6 1.9 %source_rows.1.own_hbm = bf16[32,4096]{1,0:T(8,128)(2,1)} custom-call(bf16[16,4096]{1,0:T(8,128)(2,1)} %samples_hbm.1, f32[3,4096]{1,0:T(4,128)} %coords_hbm.3, f32[1,4096]{1,0:T(1,128)} %bitcast.12, f32[1,4096]{1,0:T(1,128)} %bitcast.13), custom_call_target="tpu_custom_call" | custom-call | tf_op jit(solution)/shard_map/source_rows/pallas_call | solution.py:93
  2.6 3.7 %collective-permute-start.1 = (bf16[32,4096]{1,0:T(8,128)(2,1)}, bf16[32,4096]{1,0:T(8,128)(2,1)S(1)}, u32[]{:S(2)}, u32[]{:S(2)}) collective-permute-start(bf16[32,4096]{1,0:T(8,128)(2,1)} %source_rows.1.own_hbm), channel_id=1, source_target_pairs={{4,0},{8,4},{12,8},{16,12},{20,16},{24,20},{28,24},{32,28},{36,32}... | collective-permute-start | bytes 786440 | tf_op jit(solution)/shard_map/ppermute | solution.py:474
  6.2 1.9 %collective-permute-start = (bf16[32,4096]{1,0:T(8,128)(2,1)}, bf16[32,4096]{1,0:T(8,128)(2,1)S(1)}, u32[]{:S(2)}, u32[]{:S(2)}) collective-permute-start(bf16[32,4096]{1,0:T(8,128)(2,1)} %source_rows.1.own_hbm), channel_id=1, source_target_pairs={{0,4},{4,8},{8,12},{12,16},{16,20},{20,24},{24,28},{28,32},{32,36}... | collective-permute-start | bytes 786440 | tf_op jit(solution)/shard_map/ppermute | solution.py:473
  8.2 3.2 %send_rows.1 = bf16[384,8,128]{2,1,0:T(8,128)(2,1)} custom-call(s32[2,128]{1,0:T(2,128)} %bitcast.14, s32[1,128]{1,0:T(1,128)} %bitcast.15, bf16[32,4096]{1,0:T(8,128)(2,1)} %source_rows.1.own_hbm, bf16[16,64,256]{2,1,0:T(8,128)(2,1)} %basis_hbm.3, bf16[8,2,64,64]{3,2,1,0:T(8,128)(2,1)} %transfer_hbm.3), custom_call_target="tpu_custom_call" | custom-call | tf_op jit(solution)/shard_map/send_rows/pallas_call | solution.py:179
  11.4 0.0 collective-permute-done.1.high_hbm
  11.4 0.0 copy-start.1
  11.4 4.8 %collective-permute-done.low_hbm = bf16[32,4096]{1,0:T(8,128)(2,1)S(1)} collective-permute-done((bf16[32,4096]{1,0:T(8,128)(2,1)}, bf16[32,4096]{1,0:T(8,128)(2,1)S(1)}, u32[]{:S(2)}, u32[]{:S(2)}) %collective-permute-start) | collective-permute-done | bytes 262176 | tf_op jit(solution)/shard_map/ppermute | solution.py:473
  16.2 0.0 copy-start.2
  16.2 17.8 %all-to-all-start = ((bf16[128,24,128]{2,1,0:T(8,128)(2,1)}), bf16[128,24,128]{2,1,0:T(8,128)(2,1)S(1)}, u32[]{:S(2)}, u32[]{:S(2)}) async-start(bf16[128,24,128]{2,1,0:T(8,128)(2,1)} %bitcast.11), calls=%async_computation | async-start | bytes 1572864 | tf_op jit(solution)/shard_map/all_to_all | solution.py:479
  34.0 0.0 copy-done.1
  34.0 0.0 copy-done.2
  34.0 28.2 %near_field.1.near_hbm = f32[16,4096]{1,0:T(8,128)} custom-call(s32[1]{0:T(128)} %bitcast.6.first_ref, s32[16,16]{1,0:T(8,128)} %list_hbm.1, f32[3,4096]{1,0:T(4,128)} %coords_hbm.3, bf16[32,4096]{1,0:T(8,128)(2,1)} %source_rows.1.own_hbm, bf16[32,4096]{1,0:T(8,128)(2,1)} %copy-done.2, bf16[32,4096]{1,0:T(8,128)(2,1)} %copy-done.1), custom_call_target="tpu_custom_call" | custom-call | flops 17179869184 | bytes 4194304 | tf_op jit(solution)/shard_map/near_field/pallas_call | solution.py:274
  62.2 16.0 %all-to-all-done = bf16[128,24,128]{2,1,0:T(8,128)(2,1)S(1)} async-done(((bf16[128,24,128]{2,1,0:T(8,128)(2,1)}), bf16[128,24,128]{2,1,0:T(8,128)(2,1)S(1)}, u32[]{:S(2)}, u32[]{:S(2)}) %all-to-all-start) | async-done | bytes 786464 | tf_op jit(solution)/shard_map/all_to_all | solution.py:479
  78.2 0.0 copy-start
  78.2 0.9 copy-done
  79.1 5.0 %far_field.1 = (bf16[16,4096]{1,0:T(8,128)(2,1)}, bf16[4,16,4096]{2,1,0:T(8,128)(2,1)}) custom-call(s32[16,16]{1,0:T(8,128)} %fine_list_hbm.1, s32[8,16]{1,0:T(8,128)} %coarse_list_hbm.1, bf16[384,8,128]{2,1,0:T(8,128)(2,1)} %bitcast.10, bf16[16,16,64,64]{3,2,1,0:T(8,128)(2,1)} %fine_hbm.1, bf16[8,16,64,64]{3,2,1,0:T(8,128)(2,1)} %coarse_hbm.1, ...), custom_call_target="tpu_custom_call" | custom-call | tf_op jit(solution)/shard_map/far_field/pallas_call | solution.py:406
  84.2 4.5 %all-to-all-start.1 = ((bf16[4,16,4096]{2,1,0:T(8,128)(2,1)}), bf16[4,16,4096]{2,1,0:T(8,128)(2,1)S(1)}, u32[]{:S(2)}, u32[]{:S(2)}) async-start(bf16[4,16,4096]{2,1,0:T(8,128)(2,1)} %get-tuple-element.11), calls=%async_computation.1 | async-start | bytes 1048576 | tf_op jit(solution)/shard_map/all_to_all | solution.py:488
  88.6 10.2 %all-to-all-done.1 = bf16[4,16,4096]{2,1,0:T(8,128)(2,1)S(1)} async-done(((bf16[4,16,4096]{2,1,0:T(8,128)(2,1)}), bf16[4,16,4096]{2,1,0:T(8,128)(2,1)S(1)}, u32[]{:S(2)}, u32[]{:S(2)}) %all-to-all-start.1) | async-done | bytes 524320 | tf_op jit(solution)/shard_map/all_to_all | solution.py:488
  98.8 0.9 gram.1
Async XLA Ops:
  2.6 8.8 %collective-permute-start.1 = (bf16[32,4096]{1,0:T(8,128)(2,1)}, bf16[32,4096]{1,0:T(8,128)(2,1)S(1)}, u32[]{:S(2)}, u32[]{:S(2)}) collective-permute-start(bf16[32,4096]{1,0:T(8,128)(2,1)} %source_rows.1.own_hbm), channel_id=1, source_target_pairs={{4,0},{8,4},{12,8},{16,12},{20,16},{24,20},{28,24},{32,28},{36,32}... | collective-permute-start | bytes 786440 | tf_op jit(solution)/shard_map/ppermute | solution.py:474
  6.2 10.0 %collective-permute-start = (bf16[32,4096]{1,0:T(8,128)(2,1)}, bf16[32,4096]{1,0:T(8,128)(2,1)S(1)}, u32[]{:S(2)}, u32[]{:S(2)}) collective-permute-start(bf16[32,4096]{1,0:T(8,128)(2,1)} %source_rows.1.own_hbm), channel_id=1, source_target_pairs={{0,4},{4,8},{8,12},{12,16},{16,20},{20,24},{24,28},{28,32},{32,36}... | collective-permute-start | bytes 786440 | tf_op jit(solution)/shard_map/ppermute | solution.py:473
  11.4 22.6 %copy-start.1 = (bf16[32,4096]{1,0:T(8,128)(2,1)}, bf16[32,4096]{1,0:T(8,128)(2,1)S(1)}, u32[]{:S(2)}) copy-start(bf16[32,4096]{1,0:T(8,128)(2,1)S(1)} %collective-permute-done.1.high_hbm) | copy-start | bytes 786436
  16.2 17.8 %copy-start.2 = (bf16[32,4096]{1,0:T(8,128)(2,1)}, bf16[32,4096]{1,0:T(8,128)(2,1)S(1)}, u32[]{:S(2)}) copy-start(bf16[32,4096]{1,0:T(8,128)(2,1)S(1)} %collective-permute-done.low_hbm) | copy-start | bytes 786436
  16.2 62.0 %all-to-all-start = ((bf16[128,24,128]{2,1,0:T(8,128)(2,1)}), bf16[128,24,128]{2,1,0:T(8,128)(2,1)S(1)}, u32[]{:S(2)}, u32[]{:S(2)}) async-start(bf16[128,24,128]{2,1,0:T(8,128)(2,1)} %bitcast.11), calls=%async_computation | async-start | bytes 1572864 | tf_op jit(solution)/shard_map/all_to_all | solution.py:479
  78.2 0.9 copy-start
  84.2 14.6 %all-to-all-start.1 = ((bf16[4,16,4096]{2,1,0:T(8,128)(2,1)}), bf16[4,16,4096]{2,1,0:T(8,128)(2,1)S(1)}, u32[]{:S(2)}, u32[]{:S(2)}) async-start(bf16[4,16,4096]{2,1,0:T(8,128)(2,1)} %get-tuple-element.11), calls=%async_computation.1 | async-start | bytes 1048576 | tf_op jit(solution)/shard_map/all_to_all | solution.py:488
